TPU v7x, 512 devices: a whole 4x8x8 slice. The times are simulated.
512 devices in a mesh: tile: 32 (over y, x), tm: 16 (over z, core).
Axes of the slice: x: 4, y: 8, z: 8, core: 2. Of those that a mesh axis runs over, the one named last changes fastest.
Arguments:
- movie: bfloat16 [256, 256, 4096], P('tm', None, 'tile'), may hold values from -6 to 6
- omega: bfloat16 [2, 32, 32, 256], P(None, 'tile', None, 'tm'), may hold values from -0.375 to 0.375
- time_taps: bfloat16 [17], replicated, may hold values from 0.019897461 to 0.099609375
- space_taps: bfloat16 [17], replicated, may hold values from 0.099609375 to 0.29882812
Outputs:
- basis: float32 [32, 256, 4096], P(None, 'tm', 'tile')
- coefficients: float32 [2, 32, 32, 256], P(None, 'tile', None, 'tm')
All inputs are finite; a program needn't handle non-finite values.
Results may differ from a plain program's by a relative error of at most 0.024.
Values may be sent and summed in bfloat16 or wider, within the bound.
A program may use at most 64 MiB of HBM per device.

v0:
```python
import math
import jax
import jax.numpy as jnp
from jax import lax
from jax.sharding import PartitionSpec as P

H = 128
TY = 2


def with_halo(block, sides, width):
    for axis, dim in sides:
        count = lax.axis_size(axis)
        forward = [(i, i + 1) for i in range(count - 1)]
        backward = [(target, source) for source, target in forward]
        low = lax.ppermute(
            lax.slice_in_dim(block, block.shape[dim] - width, None, axis=dim), axis, forward
        )
        high = lax.ppermute(lax.slice_in_dim(block, 0, width, axis=dim), axis, backward)
        block = jnp.concatenate([low, block, high], axis=dim)
    return block


def band(tap_row, out_count, in_count, offset_by):
    row_ids = lax.broadcasted_iota(jnp.int32, (out_count, in_count), 0)
    col_ids = lax.broadcasted_iota(jnp.int32, (out_count, in_count), 1)
    offsets = col_ids - row_ids + offset_by
    picks = jnp.arange(tap_row.shape[0], dtype=jnp.int32)
    hits = (offsets[:, :, None] == picks).astype(jnp.float32)
    return jnp.sum(hits * tap_row.astype(jnp.float32), axis=2).astype(jnp.bfloat16)


def orthonormal(matrix):
    gram_block = jnp.dot(matrix, matrix.T, precision=lax.Precision.HIGHEST)
    factor_low = jnp.linalg.cholesky(gram_block)
    return jax.scipy.linalg.solve_triangular(factor_low, matrix, lower=True)


def local(movie, omega, time_taps, space_taps):
    frames, image_rows, tile_cols = movie.shape
    radius = (time_taps.shape[0] - 1) // 2
    tile_rows = H
    stack = TY
    pixels = tile_rows * tile_cols
    rank_count = omega.shape[2]
    row_share = image_rows // lax.axis_size("tm")
    time_band = band(time_taps, frames, frames + 2 * radius, 0)
    padded = with_halo(movie, (("tm", 0),), radius)
    flat_rows = padded.reshape(frames + 2 * radius, image_rows * tile_cols)
    low_time = jnp.dot(time_band, flat_rows, preferred_element_type=jnp.float32)
    centre = flat_rows[radius : radius + frames].astype(jnp.float32)
    temporal = (centre - low_time).astype(jnp.bfloat16).reshape(frames, image_rows, tile_cols)
    temporal = with_halo(temporal, (("tile", 2),), radius)
    across = band(space_taps, tile_cols, tile_cols + 2 * radius, 0).T
    smooth_x = jnp.dot(temporal, across, preferred_element_type=jnp.float32).astype(jnp.bfloat16)
    down_band = band(space_taps, image_rows, image_rows, radius)
    lowpass = jnp.einsum("ab,fbw->faw", down_band, smooth_x, preferred_element_type=jnp.float32)
    centre_z = temporal[:, :, radius : radius + tile_cols].astype(jnp.float32)
    filtered = (centre_z - lowpass).astype(jnp.bfloat16).reshape(frames, stack, pixels)
    row_start = lax.axis_index("tm") * row_share

    def to_image(tiled):
        shaped = tiled.reshape(stack, rank_count, tile_rows, tile_cols)
        return jnp.transpose(shaped, (1, 0, 2, 3)).reshape(rank_count, image_rows, tile_cols)

    def subspace(partial_value):
        summed = lax.psum(partial_value.astype(jnp.bfloat16), "tm").astype(jnp.float32)
        basis_all = jax.vmap(orthonormal)(summed)
        own_rows = lax.dynamic_slice_in_dim(to_image(basis_all), row_start, row_share, 1)
        return (basis_all.astype(jnp.bfloat16), own_rows)

    omega_local = omega[:, 0]
    sketch = jnp.einsum("tkf,ftp->tkp", omega_local, filtered, preferred_element_type=jnp.float32)
    first_basis, unused_rows = subspace(sketch)
    loadings = jnp.einsum(
        "ftp,tkp->ftk", filtered, first_basis, preferred_element_type=jnp.float32
    ).astype(jnp.bfloat16)
    refined = jnp.einsum("ftk,ftp->tkp", loadings, filtered, preferred_element_type=jnp.float32)
    final_basis, final_rows = subspace(refined)
    coefficients = jnp.einsum(
        "tkp,ftp->tkf", final_basis, filtered, preferred_element_type=jnp.float32
    )
    return (final_rows * math.sqrt(pixels), coefficients[:, None])


def solution(mesh):
    in_specs = (P("tm", None, "tile"), P(None, "tile", None, "tm"), P(), P())
    out_specs = (P(None, "tm", "tile"), P(None, "tile", None, "tm"))
    return jax.shard_map(local, mesh=mesh, in_specs=in_specs, out_specs=out_specs, check_vma=False)
```

profile of v0, /device:TPU:1, one launch (start us, length us, event | category | flops | bytes accessed | tf_op | source)
XLA Modules:
  0.0 342.5 jit_solution(9455576074152000294)
XLA Ops:
  7.2 1.4 fusion.46
  8.6 5.4 %collective-permute-start = (bf16[8,256,128]{2,1,0:T(8,128)(2,1)S(1)}, bf16[8,256,128]{2,1,0:T(8,128)(2,1)S(1)}, u32[]{:S(2)}, u32[]{:S(2)}) collective-permute-start(bf16[8,256,128]{2,1,0:T(8,128)(2,1)S(1)} %get-tuple-element.14), channel_id=1, source_target_pairs={{0,1},{1,2},{2,3},{3,4},{4,5},{5,6},{6,7},{7,8},{8,9},{9,10},{10,1... | collective-permute-start | bytes 1572872 | tf_op jit(solution)/shard_map/ppermute | solution.py:16
  14.0 4.7 %collective-permute-start.1 = (bf16[8,256,128]{2,1,0:T(8,128)(2,1)S(1)}, bf16[8,256,128]{2,1,0:T(8,128)(2,1)S(1)}, u32[]{:S(2)}, u32[]{:S(2)}) collective-permute-start(bf16[8,256,128]{2,1,0:T(8,128)(2,1)S(1)} %get-tuple-element.15), channel_id=1, source_target_pairs={{1,0},{2,1},{3,2},{4,3},{5,4},{6,5},{7,6},{8,7},{9,8},{10,9},{11,1... | collective-permute-start | bytes 1572872 | tf_op jit(solution)/shard_map/ppermute | solution.py:19
  19.2 0.5 select_reduce_fusion
  19.7 0.5 collective-permute-done
  20.1 4.4 %collective-permute-done.1 = bf16[8,256,128]{2,1,0:T(8,128)(2,1)S(1)} collective-permute-done((bf16[8,256,128]{2,1,0:T(8,128)(2,1)S(1)}, bf16[8,256,128]{2,1,0:T(8,128)(2,1)S(1)}, u32[]{:S(2)}, u32[]{:S(2)}) %collective-permute-start.1) | collective-permute-done | bytes 524320 | tf_op jit(solution)/shard_map/ppermute | solution.py:19
  24.5 0.2 pad_maximum_fusion
  24.8 2.3 fusion.10
  27.3 0.5 copy.38
  27.8 3.1 collective-permute-start.2
  31.0 1.3 collective-permute-start.3
  32.5 3.5 %collective-permute-done.3 = bf16[16,256,8]{1,2,0:T(8,128)(2,1)S(1)} collective-permute-done((bf16[16,256,8]{1,2,0:T(8,128)(2,1)S(1)}, bf16[16,256,8]{1,2,0:T(8,128)(2,1)S(1)}, u32[]{:S(2)}, u32[]{:S(2)}) %collective-permute-start.3) | collective-permute-done | bytes 65568 | tf_op jit(solution)/shard_map/ppermute | solution.py:19
  36.0 1.5 fusion.7
  37.5 0.7 copy.43
  38.2 0.3 reshape.57
  38.5 2.6 fusion.1
  41.2 127.3 %all-reduce.3.cloned.1.call-done = bf16[2,32,16384]{2,1,0:T(8,128)(2,1)} async-done(((bf16[2,32,16384]{2,1,0:T(8,128)(2,1)}), bf16[2,32,16384]{2,1,0:T(8,128)(2,1)}) %all-reduce.3.cloned.1.call-update) | async-done | bytes 2097168 | tf_op jit(solution)/shard_map/psum | solution.py:67
  168.6 3.0 fusion.47
  171.7 6.0 %custom-call.8 = f32[2,32,32]{2,1,0:T(8,128)S(1)} custom-call(f32[2,32,32]{2,1,0:T(8,128)S(1)} %fusion.40), custom_call_target="Cholesky" | custom-call | tf_op jit(solution)/shard_map/vmap(jit(cholesky))/cholesky | solution.py:35
  178.0 4.9 %custom-call.9 = f32[2,1,32,32]{2,3,1,0:T(8,128)S(1)} custom-call(f32[2,1,32,32]{3,2,1,0:T(8,128)S(1)} %select_bitcast_fusion.1), custom_call_target="InvertDiagBlocksLowerTriangular" | custom-call | tf_op jit(solution)/shard_map/vmap(jit(_solve_triangular))/triangular_solve | solution.py:36
  182.9 4.8 %convolution_convert_fusion.1 = bf16[2,32,16384]{2,1,0:T(8,128)(2,1)} fusion(bf16[2,32,16384]{2,1,0:T(8,128)(2,1)S(1)} %copy-done.2, f32[2,1,32,32]{2,3,1,0:T(8,128)S(1)} %custom-call.9), kind=kOutput, calls=%fused_computation.3 | convolution fusion | flops 404750336 | bytes 4202496 | tf_op jit(solution)/shard_map/vmap(jit(_solve_triangular))/triangular_solve | solution.py:36
  187.7 5.3 %convolution_convert_fusion = bf16[2,32,16384]{2,1,0:T(8,128)(2,1)} fusion(bf16[2,32,16384]{2,1,0:T(8,128)(2,1)} %convolution_convert_fusion.1, bf16[16,2,16384]{2,1,0:T(2,128)(2,1)S(1)} %reshape.57), kind=kOutput, calls=%fused_computation.2 | convolution fusion | flops 68158464 | bytes 5242880 | tf_op jit(solution)/shard_map/ftk,ftp->tkp/dot_general | solution.py:78
  193.0 120.7 %all-reduce.5.cloned.1.call-done = bf16[2,32,16384]{2,1,0:T(8,128)(2,1)} async-done(((bf16[2,32,16384]{2,1,0:T(8,128)(2,1)}), bf16[2,32,16384]{2,1,0:T(8,128)(2,1)}) %all-reduce.5.cloned.1.call-update) | async-done | bytes 2097168 | tf_op jit(solution)/shard_map/psum | solution.py:67
  313.7 3.0 fusion.48
  316.8 5.9 %custom-call.10 = f32[2,32,32]{2,1,0:T(8,128)S(1)} custom-call(f32[2,32,32]{2,1,0:T(8,128)S(1)} %fusion.38), custom_call_target="Cholesky" | custom-call | tf_op jit(solution)/shard_map/vmap(jit(cholesky))/cholesky | solution.py:35
  322.9 4.9 %custom-call.11 = f32[2,1,32,32]{2,3,1,0:T(8,128)S(1)} custom-call(f32[2,1,32,32]{3,2,1,0:T(8,128)S(1)} %select_bitcast_fusion), custom_call_target="InvertDiagBlocksLowerTriangular" | custom-call | tf_op jit(solution)/shard_map/vmap(jit(_solve_triangular))/triangular_solve | solution.py:36
  327.9 3.9 %fusion.2 = f32[2,32,16384]{2,1,0:T(8,128)S(1)} fusion(bf16[2,32,16384]{2,1,0:T(8,128)(2,1)S(1)} %copy-done.1, f32[2,1,32,32]{2,3,1,0:T(8,128)S(1)} %custom-call.11), kind=kOutput, calls=%fused_computation.9 | convolution fusion | flops 403701760 | bytes 6299648 | tf_op jit(solution)/shard_map/vmap(jit(_solve_triangular))/triangular_solve | solution.py:36
  331.7 1.5 fusion.23
  333.2 0.7 copy.60
  333.9 0.5 bitcast_bitcast_fusion
  334.4 0.5 copy.51
  334.9 0.7 dynamic-slice_multiply_fusion
  (39 shorter events, 1.5 us)
Async XLA Ops:
  7.2 31.3 %copy-start = (bf16[2,1,32,16]{2,3,1,0:T(8,128)(2,1)S(1)}, bf16[2,1,32,16]{2,3,1,0:T(8,128)(2,1)}, u32[]{:S(2)}) copy-start(bf16[2,1,32,16]{2,3,1,0:T(8,128)(2,1)} %param.8) | copy-start | bytes 6148
  7.2 11.6 %copy-start.3 = (bf16[16,256,128]{2,1,0:T(8,128)(2,1)S(1)}, bf16[16,256,128]{2,1,0:T(8,128)(2,1)}, u32[]{:S(2)}) copy-start(bf16[16,256,128]{2,1,0:T(8,128)(2,1)} %param.7) | copy-start | bytes 3145732
  7.2 161.4 %all-reduce.3.cloned.1.call-start = ((), (), s32[]{:S(2)}) async-start(), calls=%async_computation | async-start | bytes 4194304 | tf_op jit(solution)/shard_map/psum | solution.py:67
  8.6 10.4 %copy-start.4 = (bf16[17]{0:T(256)(128)(2,1)S(1)}, bf16[17]{0:T(256)(128)(2,1)}, u32[]{:S(2)}) copy-start(bf16[17]{0:T(256)(128)(2,1)} %param.9) | copy-start | bytes 106
  8.6 10.4 %copy-start.5 = (bf16[17]{0:T(256)(128)(2,1)S(1)}, bf16[17]{0:T(256)(128)(2,1)}, u32[]{:S(2)}) copy-start(bf16[17]{0:T(256)(128)(2,1)} %param.10) | copy-start | bytes 106
  8.6 11.5 %collective-permute-start = (bf16[8,256,128]{2,1,0:T(8,128)(2,1)S(1)}, bf16[8,256,128]{2,1,0:T(8,128)(2,1)S(1)}, u32[]{:S(2)}, u32[]{:S(2)}) collective-permute-start(bf16[8,256,128]{2,1,0:T(8,128)(2,1)S(1)} %get-tuple-element.14), channel_id=1, source_target_pairs={{0,1},{1,2},{2,3},{3,4},{4,5},{5,6},{6,7},{7,8},{8,9},{9,10},{10,1... | collective-permute-start | bytes 1572872 | tf_op jit(solution)/shard_map/ppermute | solution.py:16
  14.0 10.5 %collective-permute-start.1 = (bf16[8,256,128]{2,1,0:T(8,128)(2,1)S(1)}, bf16[8,256,128]{2,1,0:T(8,128)(2,1)S(1)}, u32[]{:S(2)}, u32[]{:S(2)}) collective-permute-start(bf16[8,256,128]{2,1,0:T(8,128)(2,1)S(1)} %get-tuple-element.15), channel_id=1, source_target_pairs={{1,0},{2,1},{3,2},{4,3},{5,4},{6,5},{7,6},{8,7},{9,8},{10,9},{11,1... | collective-permute-start | bytes 1572872 | tf_op jit(solution)/shard_map/ppermute | solution.py:19
  27.8 4.6 %collective-permute-start.2 = (bf16[16,256,8]{1,2,0:T(8,128)(2,1)S(1)}, bf16[16,256,8]{1,2,0:T(8,128)(2,1)S(1)}, u32[]{:S(2)}, u32[]{:S(2)}) collective-permute-start(bf16[16,256,8]{1,2,0:T(8,128)(2,1)S(1)} %get-tuple-element.12), channel_id=1, source_target_pairs={{0,16},{16,32},{32,48},{48,64},{64,80},{80,96},{96,112},{112,128},... | collective-permute-start | bytes 196616 | tf_op jit(solution)/shard_map/ppermute | solution.py:16
  31.0 5.0 %collective-permute-start.3 = (bf16[16,256,8]{1,2,0:T(8,128)(2,1)S(1)}, bf16[16,256,8]{1,2,0:T(8,128)(2,1)S(1)}, u32[]{:S(2)}, u32[]{:S(2)}) collective-permute-start(bf16[16,256,8]{1,2,0:T(8,128)(2,1)S(1)} %get-tuple-element.13), channel_id=1, source_target_pairs={{16,0},{32,16},{48,32},{64,48},{80,64},{96,80},{112,96},{128,112},... | collective-permute-start | bytes 196616 | tf_op jit(solution)/shard_map/ppermute | solution.py:19
  41.2 272.5 %all-reduce.5.cloned.1.call-start = ((), (), s32[]{:S(2)}) async-start(), calls=%async_computation.1 | async-start | bytes 4194304 | tf_op jit(solution)/shard_map/psum | solution.py:67
  168.6 14.3 %copy-start.2 = (bf16[2,32,16384]{2,1,0:T(8,128)(2,1)S(1)}, bf16[2,32,16384]{2,1,0:T(8,128)(2,1)}, u32[]{:S(2)}) copy-start(bf16[2,32,16384]{2,1,0:T(8,128)(2,1)} %all-reduce.3.cloned.1.call-done) | copy-start | bytes 6291460
  313.7 14.2 %copy-start.1 = (bf16[2,32,16384]{2,1,0:T(8,128)(2,1)S(1)}, bf16[2,32,16384]{2,1,0:T(8,128)(2,1)}, u32[]{:S(2)}) copy-start(bf16[2,32,16384]{2,1,0:T(8,128)(2,1)} %all-reduce.5.cloned.1.call-done) | copy-start | bytes 6291460
Sparse Core Ops, SparseCore 0:
  41.3 127.2 all-reduce.2
  193.1 120.5 all-reduce.4
where the time goes:
time: 343 us; the launch traced here: 342 us
  waiting for transfers between devices  256 us (75%)
  matrix products  27.9 us (8%)
  other arithmetic  24.2 us (7%)
  starting transfers between devices  14.6 us (4%)
  between operations  14.3 us (4%)
  local copies, waits for them, and re-layouts  4.95 us (1%)
    psum x2, waiting for transfers between devices, subspace(): lax.psum(partial_value.astype(jnp.bfloat16), 'tm').astype(jnp.float32)  248 us
    another operation x7, other arithmetic, orthonormal(): factor_low = jnp.linalg.cholesky(gram_block)  12.2 us
    another operation x5, other arithmetic, orthonormal(): return jax.scipy.linalg.solve_triangular(factor_low, matrix, lower=True)  9.99 us
    another operation x2, matrix products, orthonormal(): return jax.scipy.linalg.solve_triangular(factor_low, matrix, lower=True)  8.65 us
    ppermute x2, starting transfers between devices, with_halo(): lax.ppermute(lax.slice_in_dim(block, block.shape[dim] - width, None, axis...  8.51 us
    ppermute x2, waiting for transfers between devices, with_halo(): lax.ppermute(lax.slice_in_dim(block, 0, width, axis=dim), axis, backward)  7.9 us
  transfers between devices with their start and end apart: 6, of which 5 were waited for; matrix products, arithmetic and copies ran while one was open for 0% of the time, Pallas kernels for 0%

commit v1 on v0

--- a/solution.py
+++ b/solution.py
@@ -64,7 +64,9 @@
         return jnp.transpose(shaped, (1, 0, 2, 3)).reshape(rank_count, image_rows, tile_cols)
 
     def subspace(partial_value):
-        summed = lax.psum(partial_value.astype(jnp.bfloat16), "tm").astype(jnp.float32)
+        summed = jnp.sum(lax.all_gather(partial_value.astype(jnp.bfloat16), "tm"), axis=0).astype(
+            jnp.float32
+        )
         basis_all = jax.vmap(orthonormal)(summed)
         own_rows = lax.dynamic_slice_in_dim(to_image(basis_all), row_start, row_share, 1)
         return (basis_all.astype(jnp.bfloat16), own_rows)

time: 343 us -> 474 us (1.38)
  waiting for transfers between devices: 256 us -> 369 us
  other arithmetic: 24.2 us -> 47.5 us
    all_gather x0 -> x2, waiting for transfers between devices: none -> 361 us  [subspace(): lax.all_gather(partial_value.astype(jnp.bfloat16), 'tm')]
    psum x2 -> x0, waiting for transfers between devices: 248 us -> none  [subspace(): lax.psum(partial_value.astype(jnp.bfloat16), 'tm').astype(jnp.float32)]
    reduce_sum x0 -> x2, other arithmetic: none -> 23.3 us  [subspace(): jnp.sum(lax.all_gather(partial_value.astype(jnp.bfloat16), 'tm'), axis=0)]
    dot_general x2, matrix products: 6.08 us -> 1.34 us  [orthonormal(): gram_block = jnp.dot(matrix, matrix.T, precision=lax.Precision.HIGHEST)]
where the time goes in v1:
time: 474 us
  waiting for transfers between devices  369 us (78%)
  other arithmetic  47.5 us (10%)
  matrix products  23.2 us (5%)
  starting transfers between devices  14.8 us (3%)
  between operations  14.4 us (3%)
  local copies, waits for them, and re-layouts  4.94 us (1%)
    all_gather x2, waiting for transfers between devices, subspace(): lax.all_gather(partial_value.astype(jnp.bfloat16), 'tm')  361 us
    reduce_sum x2, other arithmetic, subspace(): jnp.sum(lax.all_gather(partial_value.astype(jnp.bfloat16), 'tm'), axis=0)  23.3 us
    another operation x7, other arithmetic, orthonormal(): factor_low = jnp.linalg.cholesky(gram_block)  12 us
    another operation x5, other arithmetic, orthonormal(): return jax.scipy.linalg.solve_triangular(factor_low, matrix, lower=True)  10.2 us
  transfers between devices with their start and end apart: 6, of which 5 were waited for; matrix products, arithmetic and copies ran while one was open for 0% of the time, Pallas kernels for 0%

profile of v1, /device:TPU:1, one launch (start us, length us, event | category | flops | bytes accessed | tf_op | source)
XLA Modules:
  0.0 473.8 jit_solution(10413780454010770378)
XLA Ops:
  7.2 1.4 fusion.46
  8.6 5.4 %collective-permute-start = (bf16[8,256,128]{2,1,0:T(8,128)(2,1)S(1)}, bf16[8,256,128]{2,1,0:T(8,128)(2,1)S(1)}, u32[]{:S(2)}, u32[]{:S(2)}) collective-permute-start(bf16[8,256,128]{2,1,0:T(8,128)(2,1)S(1)} %get-tuple-element.14), channel_id=1, source_target_pairs={{0,1},{1,2},{2,3},{3,4},{4,5},{5,6},{6,7},{7,8},{8,9},{9,10},{10,1... | collective-permute-start | bytes 1572872 | tf_op jit(solution)/shard_map/ppermute | solution.py:16
  14.0 4.7 collective-permute-start.1
  19.2 0.5 select_reduce_fusion
  19.7 0.5 collective-permute-done
  20.1 4.4 collective-permute-done.1
  24.8 2.3 fusion.10
  27.3 0.5 copy.38
  27.8 3.1 collective-permute-start.2
  31.0 1.3 collective-permute-start.3
  32.5 3.5 collective-permute-done.3
  36.0 1.5 fusion.7
  37.5 0.7 copy.43
  38.5 2.7 fusion.1
  41.4 184.6 %all-gather.5.cloned.1.call-done = bf16[32,32,16384]{2,1,0:T(8,128)(2,1)} async-done(((bf16[2,32,16384]{2,1,0:T(8,128)(2,1)}), bf16[32,32,16384]{2,1,0:T(8,128)(2,1)}) %all-gather.5.cloned.1.call-update) | async-done | bytes 33554448 | tf_op jit(solution)/shard_map/all_gather | solution.py:67
  226.1 11.6 %reduce_sum.54 = bf16[2,32,16384]{2,1,0:T(8,128)(2,1)S(1)} reduce(bf16[16,2,32,16384]{3,2,1,0:T(8,128)(2,1)} %bitcast.76, bf16[]{:T(256)} %constant.48.clone.1), dimensions={0}, to_apply=%region_3.0 | reduce | flops 15728640 | bytes 35651584 | tf_op jit(solution)/shard_map/reduce_sum | solution.py:67
  237.7 0.7 fusion.47
  238.5 5.9 %custom-call.8 = f32[2,32,32]{2,1,0:T(8,128)S(1)} custom-call(f32[2,32,32]{2,1,0:T(8,128)S(1)} %fusion.40), custom_call_target="Cholesky" | custom-call | tf_op jit(solution)/shard_map/vmap(jit(cholesky))/cholesky | solution.py:35
  244.6 4.9 %custom-call.9 = f32[2,1,32,32]{2,3,1,0:T(8,128)S(1)} custom-call(f32[2,1,32,32]{3,2,1,0:T(8,128)S(1)} %select_bitcast_fusion.1), custom_call_target="InvertDiagBlocksLowerTriangular" | custom-call | tf_op jit(solution)/shard_map/vmap(jit(_solve_triangular))/triangular_solve | solution.py:36
  249.5 4.8 %convolution_convert_fusion.1 = bf16[2,32,16384]{2,1,0:T(8,128)(2,1)} fusion(bf16[2,32,16384]{2,1,0:T(8,128)(2,1)S(1)} %reduce_sum.54, f32[2,1,32,32]{2,3,1,0:T(8,128)S(1)} %custom-call.9), kind=kOutput, calls=%fused_computation.3 | convolution fusion | flops 404750336 | bytes 4202496 | tf_op jit(solution)/shard_map/vmap(jit(_solve_triangular))/triangular_solve | solution.py:36
  254.3 5.2 %convolution_convert_fusion = bf16[2,32,16384]{2,1,0:T(8,128)(2,1)} fusion(bf16[2,32,16384]{2,1,0:T(8,128)(2,1)} %convolution_convert_fusion.1, bf16[16,2,16384]{2,1,0:T(2,128)(2,1)S(1)} %reshape.57), kind=kOutput, calls=%fused_computation.2 | convolution fusion | flops 68158464 | bytes 5242880 | tf_op jit(solution)/shard_map/ftk,ftp->tkp/dot_general | solution.py:80
  259.6 175.9 %all-gather.7.cloned.1.call-done = bf16[32,32,16384]{2,1,0:T(8,128)(2,1)} async-done(((bf16[2,32,16384]{2,1,0:T(8,128)(2,1)}), bf16[32,32,16384]{2,1,0:T(8,128)(2,1)}) %all-gather.7.cloned.1.call-update) | async-done | bytes 33554448 | tf_op jit(solution)/shard_map/all_gather | solution.py:67
  435.5 11.6 %reduce_sum.55 = bf16[2,32,16384]{2,1,0:T(8,128)(2,1)S(1)} reduce(bf16[16,2,32,16384]{3,2,1,0:T(8,128)(2,1)} %bitcast.75, bf16[]{:T(256)} %constant.48.clone.1), dimensions={0}, to_apply=%region_6.9 | reduce | flops 15728640 | bytes 35651584 | tf_op jit(solution)/shard_map/reduce_sum | solution.py:67
  447.2 0.7 fusion.48
  447.9 5.9 %custom-call.10 = f32[2,32,32]{2,1,0:T(8,128)S(1)} custom-call(f32[2,32,32]{2,1,0:T(8,128)S(1)} %fusion.38), custom_call_target="Cholesky" | custom-call | tf_op jit(solution)/shard_map/vmap(jit(cholesky))/cholesky | solution.py:35
  454.0 5.1 %custom-call.11 = f32[2,1,32,32]{2,3,1,0:T(8,128)S(1)} custom-call(f32[2,1,32,32]{3,2,1,0:T(8,128)S(1)} %select_bitcast_fusion), custom_call_target="InvertDiagBlocksLowerTriangular" | custom-call | tf_op jit(solution)/shard_map/vmap(jit(_solve_triangular))/triangular_solve | solution.py:36
  459.2 3.8 fusion.2
  463.0 1.5 fusion.23
  464.5 0.7 copy.60
  465.2 0.5 bitcast_bitcast_fusion
  465.7 0.5 copy.51
  466.2 0.7 dynamic-slice_multiply_fusion
  (39 shorter events, 2.2 us)
Async XLA Ops:
  7.2 31.3 %copy-start = (bf16[2,1,32,16]{2,3,1,0:T(8,128)(2,1)S(1)}, bf16[2,1,32,16]{2,3,1,0:T(8,128)(2,1)}, u32[]{:S(2)}) copy-start(bf16[2,1,32,16]{2,3,1,0:T(8,128)(2,1)} %param.8) | copy-start | bytes 6148
  7.2 11.6 %copy-start.2 = (bf16[16,256,128]{2,1,0:T(8,128)(2,1)S(1)}, bf16[16,256,128]{2,1,0:T(8,128)(2,1)}, u32[]{:S(2)}) copy-start(bf16[16,256,128]{2,1,0:T(8,128)(2,1)} %param.7) | copy-start | bytes 3145732
  7.2 218.9 %all-gather.5.cloned.1.call-start = ((), (), s32[]{:S(2)}) async-start(), calls=%async_computation | async-start | bytes 35651584 | tf_op jit(solution)/shard_map/all_gather | solution.py:67
  8.6 10.4 %copy-start.3 = (bf16[17]{0:T(256)(128)(2,1)S(1)}, bf16[17]{0:T(256)(128)(2,1)}, u32[]{:S(2)}) copy-start(bf16[17]{0:T(256)(128)(2,1)} %param.9) | copy-start | bytes 106
  8.6 10.4 %copy-start.4 = (bf16[17]{0:T(256)(128)(2,1)S(1)}, bf16[17]{0:T(256)(128)(2,1)}, u32[]{:S(2)}) copy-start(bf16[17]{0:T(256)(128)(2,1)} %param.10) | copy-start | bytes 106
  8.6 11.5 %collective-permute-start = (bf16[8,256,128]{2,1,0:T(8,128)(2,1)S(1)}, bf16[8,256,128]{2,1,0:T(8,128)(2,1)S(1)}, u32[]{:S(2)}, u32[]{:S(2)}) collective-permute-start(bf16[8,256,128]{2,1,0:T(8,128)(2,1)S(1)} %get-tuple-element.14), channel_id=1, source_target_pairs={{0,1},{1,2},{2,3},{3,4},{4,5},{5,6},{6,7},{7,8},{8,9},{9,10},{10,1... | collective-permute-start | bytes 1572872 | tf_op jit(solution)/shard_map/ppermute | solution.py:16
  14.0 10.5 %collective-permute-start.1 = (bf16[8,256,128]{2,1,0:T(8,128)(2,1)S(1)}, bf16[8,256,128]{2,1,0:T(8,128)(2,1)S(1)}, u32[]{:S(2)}, u32[]{:S(2)}) collective-permute-start(bf16[8,256,128]{2,1,0:T(8,128)(2,1)S(1)} %get-tuple-element.15), channel_id=1, source_target_pairs={{1,0},{2,1},{3,2},{4,3},{5,4},{6,5},{7,6},{8,7},{9,8},{10,9},{11,1... | collective-permute-start | bytes 1572872 | tf_op jit(solution)/shard_map/ppermute | solution.py:19
  27.8 4.6 collective-permute-start.2
  31.0 5.0 %collective-permute-start.3 = (bf16[16,256,8]{1,2,0:T(8,128)(2,1)S(1)}, bf16[16,256,8]{1,2,0:T(8,128)(2,1)S(1)}, u32[]{:S(2)}, u32[]{:S(2)}) collective-permute-start(bf16[16,256,8]{1,2,0:T(8,128)(2,1)S(1)} %get-tuple-element.13), channel_id=1, source_target_pairs={{16,0},{32,16},{48,32},{64,48},{80,64},{96,80},{112,96},{128,112},... | collective-permute-start | bytes 196616 | tf_op jit(solution)/shard_map/ppermute | solution.py:19
  41.2 394.4 %all-gather.7.cloned.1.call-start = ((), (), s32[]{:S(2)}) async-start(), calls=%async_computation.1 | async-start | bytes 35651584 | tf_op jit(solution)/shard_map/all_gather | solution.py:67
  465.7 1.2 copy-start.1
Sparse Core Ops, SparseCore 0:
  41.3 184.7 all-gather.4
  259.7 175.7 all-gather.6
